TPU v7x, 32 devices: a whole 2x2x4 slice. The times are simulated.
32 devices in a mesh: tm: 16 (over z, y, x), space: 2 (over core).
Axes of the slice: x: 2, y: 2, z: 4, core: 2. Of those that a mesh axis runs over, the one named last changes fastest.
Arguments:
- source: float32 [64, 64, 512], P('tm', None, 'space'), may hold values from -3 to 3
- initial: float32 [64, 512], P(None, 'space'), may hold values from -6 to 6
- mass: float32 [64, 512], P(None, 'space'), may hold values from 0.8 to 1.25
- inverses: bfloat16 [3, 64, 64, 512], P(None, None, None, 'space'), may hold values from -0.3 to 1, as said below
- couplings: float32 [3, 6, 16, 16], replicated, may hold values from -0.375 to 0.375
- neighbours: int32 [6, 512], P(None, 'space'), may hold values from 0 to 288, as said below
- sends: int32 [2, 32], P(None, 'space'), may hold values from 0 to 255, as said below
Outputs:
- states: float32 [64, 64, 512], P('tm', None, 'space')
Inputs may be any that keep to these rules, and one draw needn't show every extreme that they name: `neighbours`: each device's elements form a 16 x 4 x 4 block in its own order; an entry below 256 is a slot of the same device, 256 + j the j-th upper-face element of the device below, 272 + j the j-th lower-face element of the device above, 288 no neighbour. `sends`: row 0 lists the device's lower span-end elements, row 1 its upper ones, both in the same order of position on the face. `inverses`: each block is the identity scaled per node plus off-diagonal entries.
All inputs are finite; a program needn't handle non-finite values.
Results may differ from a plain program's by a relative error of at most 0.0003.
Values sent between devices are 32-bit elements; how exact they have to be, the bound alone decides.
A program may use at most 64 MiB of HBM per device.

v0:
```python
import jax
import jax.numpy as jnp
from jax import lax
from jax.sharding import PartitionSpec as P


def extended_2(block, sides, width):
    for axis, dim in sides:
        count = lax.axis_size(axis)
        forward = [(i, i + 1) for i in range(count - 1)]
        backward = [(target, source) for source, target in forward]
        low = lax.ppermute(
            lax.slice_in_dim(block, block.shape[dim] - width, None, axis=dim), axis, forward
        )
        high = lax.ppermute(lax.slice_in_dim(block, 0, width, axis=dim), axis, backward)
        block = jnp.concatenate([low, block, high], axis=dim)
    return block


def from_behind(value, axis, steps):
    count = lax.axis_size(axis)
    initial, last = (max(0, -steps), min(count, count - steps))
    return lax.ppermute(value, axis, [(source, source + steps) for source in range(initial, last)])


def trace_faces(state):
    elements = state.shape[-1]
    node_cube = state.reshape(state.shape[:-2] + (4, 4, 4, elements))
    face_sides = [
        node_cube[..., :, :, 0, :],
        node_cube[..., :, :, 3, :],
        node_cube[..., :, 0, :, :],
        node_cube[..., :, 3, :, :],
        node_cube[..., 0, :, :, :],
        node_cube[..., 3, :, :, :],
    ]
    return jnp.stack(
        [one_side.reshape(state.shape[:-2] + (16, elements)) for one_side in face_sides], axis=-3
    )


def coupling_table(coupling):
    lifting = trace_faces(jnp.eye(64, dtype=coupling.dtype))
    return jnp.einsum("fkn,fkm->nfm", lifting, coupling, precision=lax.Precision.HIGHEST).reshape(
        64, 96
    )


def selectors(neighbours, sends):
    elements = neighbours.shape[1]
    face_count = sends.shape[1]
    widest = elements + 2 * face_count + 1
    slot_ids = lax.broadcasted_iota(jnp.int32, (6, widest, elements), 1)
    picker = (slot_ids == neighbours[:, None, :]).astype(jnp.float32)
    local_ids = lax.broadcasted_iota(jnp.int32, (2, elements, face_count), 1)
    sender = (local_ids == sends[:, None, :]).astype(jnp.float32)
    return (picker, sender)


def propagate(state, inverse, mass, table, picker, sender):
    elements = state.shape[-1]
    face_count = sender.shape[2]
    traces = trace_faces(state)
    lower_out = jnp.dot(
        traces[0], sender[0], precision=lax.Precision.HIGHEST, preferred_element_type=jnp.float32
    )
    upper_out = jnp.dot(
        traces[1], sender[1], precision=lax.Precision.HIGHEST, preferred_element_type=jnp.float32
    )
    outgoing = jnp.concatenate([lower_out, upper_out], axis=1)
    widened = extended_2(outgoing, (("space", 1),), face_count)
    from_below = widened[:, :face_count]
    from_above = widened[:, 3 * face_count :]
    blank_slot = jnp.zeros((16, 1), state.dtype)
    extended = jnp.stack(
        [
            jnp.concatenate([traces[face ^ 1], from_below, from_above, blank_slot], axis=1)
            for face in range(6)
        ]
    )
    picked = jnp.einsum("fkw,fwe->fke", extended, picker, precision=lax.Precision.HIGHEST).reshape(
        96, elements
    )
    coupled = jnp.dot(
        table, picked, precision=lax.Precision.HIGHEST, preferred_element_type=jnp.float32
    )
    rhs_local = mass * state - coupled
    return jnp.sum(inverse * rhs_local[None, :, :], axis=1)


def relay(value, distance):
    return from_behind(value, "tm", distance)


def local(source, initial, mass, inverses, couplings, neighbours, sends):
    tables = [coupling_table(couplings[level_index]) for level_index in range(3)]
    picker, sender = selectors(neighbours, sends)

    def advance_level(state, level_index):
        return propagate(state, inverses[level_index], mass, tables[level_index], picker, sender)

    device = lax.axis_index("tm")
    group_place = device % 4
    groups = lax.axis_size("tm") // 4
    empty_state = jnp.zeros_like(initial)
    fine_state = empty_state
    for offset in range(1, 4):
        fine_state = advance_level(fine_state, 0) + source[offset]
    arrived = from_behind(advance_level(fine_state, 0), "tm", 1)
    residual = jnp.where(device == 0, initial, source[0] + arrived)

    def level_one_step(carried, target):
        incoming = relay(carried, 1)
        return jnp.where(group_place == target, advance_level(incoming, 1) + residual, carried)

    correction = jnp.where(group_place == 1, residual, empty_state)
    for target in (2, 3):
        correction = level_one_step(correction, target)
    relaxed = jnp.where(group_place == 0, empty_state, correction)
    coarse_rhs = jnp.where(group_place == 0, level_one_step(correction, 0), empty_state)
    forward = relay(coarse_rhs, 1)
    coarse_rhs = jnp.where(group_place == 1, forward, coarse_rhs)
    forward = relay(coarse_rhs, 2)
    coarse_rhs = jnp.where(group_place >= 2, forward, coarse_rhs)

    def chain_turn(turn_index, carried):
        incoming = from_behind(carried, "tm", 4)
        return advance_level(incoming, 2) + coarse_rhs

    coarse_value = lax.fori_loop(0, groups - 1, chain_turn, coarse_rhs)
    lifted = coarse_value
    for rank in (1, 2, 3):
        lifted = jnp.where(group_place >= rank, advance_level(lifted, 1), lifted)
    current = relaxed + lifted
    states = [current]
    for offset in range(1, 4):
        current = advance_level(current, 0) + source[offset]
        states.append(current)
    return jnp.stack(states)


def solution(mesh):
    placed = (
        P("tm", None, "space"),
        P(None, "space"),
        P(None, "space"),
        P(None, None, None, "space"),
        P(),
        P(None, "space"),
        P(None, "space"),
    )
    return jax.shard_map(
        local, mesh=mesh, in_specs=placed, out_specs=P("tm", None, "space"), check_vma=False
    )
```

profile of v0, /device:TPU:0, one launch (start us, length us, event | category | flops | bytes accessed | tf_op | source)
XLA Modules:
  0.0 218.5 jit_solution(9122074426963090510)
XLA Ops:
  0.9 2.4 %collective-permute-start.3 = (f32[16,16]{1,0:T(8,128)S(1)}, f32[16,16]{1,0:T(8,128)S(1)}, u32[]{:S(2)}, u32[]{:S(2)}) collective-permute-start(f32[16,16]{1,0:T(8,128)S(1)} %fusion.235), channel_id=1, source_target_pairs={{0,1},{2,3},{4,5},{6,7},{8,9},{10,11},{12,13},{14,15},{16,17},{18,... | collective-permute-start | bytes 3080 | tf_op jit(solution)/shard_map/ppermute | solution.py:12
  9.8 2.3 %fusion.36 = f32[64,256]{1,0:T(8,128)S(1)} fusion(f32[64,256]{1,0:T(8,128)S(1)} %fusion.56, bf16[3,64,64,256]{3,2,1,0:T(8,128)(2,1)} %param.12), kind=kLoop, calls=%fused_computation.66 | loop fusion | flops 3129344 | bytes 2228224 | tf_op jit(solution)/shard_map/reduce_sum | solution.py:88
  13.9 3.0 %collective-permute-start.5 = (f32[16,16]{1,0:T(8,128)S(1)}, f32[16,16]{1,0:T(8,128)S(1)}, u32[]{:S(2)}, u32[]{:S(2)}) collective-permute-start(f32[16,16]{1,0:T(8,128)S(1)} %fusion.251), channel_id=1, source_target_pairs={{0,1},{2,3},{4,5},{6,7},{8,9},{10,11},{12,13},{14,15},{16,17},{18,... | collective-permute-start | bytes 3080 | tf_op jit(solution)/shard_map/ppermute | solution.py:12
  23.3 3.0 %collective-permute-start.7 = (f32[16,16]{1,0:T(8,128)S(1)}, f32[16,16]{1,0:T(8,128)S(1)}, u32[]{:S(2)}, u32[]{:S(2)}) collective-permute-start(f32[16,16]{1,0:T(8,128)S(1)} %fusion.250), channel_id=1, source_target_pairs={{0,1},{2,3},{4,5},{6,7},{8,9},{10,11},{12,13},{14,15},{16,17},{18,... | collective-permute-start | bytes 3080 | tf_op jit(solution)/shard_map/ppermute | solution.py:12
  32.7 3.0 %collective-permute-start.9 = (f32[16,16]{1,0:T(8,128)S(1)}, f32[16,16]{1,0:T(8,128)S(1)}, u32[]{:S(2)}, u32[]{:S(2)}) collective-permute-start(f32[16,16]{1,0:T(8,128)S(1)} %fusion.249), channel_id=1, source_target_pairs={{0,1},{2,3},{4,5},{6,7},{8,9},{10,11},{12,13},{14,15},{16,17},{18,... | collective-permute-start | bytes 3080 | tf_op jit(solution)/shard_map/ppermute | solution.py:12
  40.3 4.2 %collective-permute-start.11 = (f32[64,256]{1,0:T(8,128)S(1)}, f32[64,256]{1,0:T(8,128)S(1)}, u32[]{:S(2)}, u32[]{:S(2)}) collective-permute-start(f32[64,256]{1,0:T(8,128)S(1)} %fusion.39), channel_id=1, source_target_pairs={{0,2},{2,4},{4,6},{6,8},{8,10},{10,12},{12,14},{14,16},{16,18},{18... | collective-permute-start | bytes 196616 | tf_op jit(solution)/shard_map/ppermute | solution.py:23
  46.5 4.3 %collective-permute-start.12 = (f32[64,256]{1,0:T(8,128)S(1)}, f32[64,256]{1,0:T(8,128)S(1)}, u32[]{:S(2)}, u32[]{:S(2)}) collective-permute-start(f32[64,256]{1,0:T(8,128)S(1)} %get-tuple-element.117), channel_id=1, source_target_pairs={{0,2},{2,4},{4,6},{6,8},{8,10},{10,12},{12,14},{14,16},{16,18},{18... | collective-permute-start | bytes 196616 | tf_op jit(solution)/shard_map/ppermute | solution.py:23
  54.4 3.0 %collective-permute-start.13 = (f32[16,16]{1,0:T(8,128)S(1)}, f32[16,16]{1,0:T(8,128)S(1)}, u32[]{:S(2)}, u32[]{:S(2)}) collective-permute-start(f32[16,16]{1,0:T(8,128)S(1)} %fusion.248), channel_id=1, source_target_pairs={{0,1},{2,3},{4,5},{6,7},{8,9},{10,11},{12,13},{14,15},{16,17},{18,... | collective-permute-start | bytes 3080 | tf_op jit(solution)/shard_map/ppermute | solution.py:12
  62.1 4.3 %collective-permute-start.15 = (f32[64,256]{1,0:T(8,128)S(1)}, f32[64,256]{1,0:T(8,128)S(1)}, u32[]{:S(2)}, u32[]{:S(2)}) collective-permute-start(f32[64,256]{1,0:T(8,128)S(1)} %add_select_fusion.1), channel_id=1, source_target_pairs={{0,2},{2,4},{4,6},{6,8},{8,10},{10,12},{12,14},{14,16},{16,18},{18... | collective-permute-start | bytes 196616 | tf_op jit(solution)/shard_map/ppermute | solution.py:23
  70.0 3.2 %collective-permute-start.16 = (f32[16,16]{1,0:T(8,128)S(1)}, f32[16,16]{1,0:T(8,128)S(1)}, u32[]{:S(2)}, u32[]{:S(2)}) collective-permute-start(f32[16,16]{1,0:T(8,128)S(1)} %fusion.247), channel_id=1, source_target_pairs={{0,1},{2,3},{4,5},{6,7},{8,9},{10,11},{12,13},{14,15},{16,17},{18,... | collective-permute-start | bytes 3080 | tf_op jit(solution)/shard_map/ppermute | solution.py:12
  77.6 5.2 %collective-permute-start.18 = (f32[64,256]{1,0:T(8,128)S(1)}, f32[64,256]{1,0:T(8,128)S(1)}, u32[]{:S(2)}, u32[]{:S(2)}) collective-permute-start(f32[64,256]{1,0:T(8,128)S(1)} %add_select_fusion), channel_id=1, source_target_pairs={{0,2},{2,4},{4,6},{6,8},{8,10},{10,12},{12,14},{14,16},{16,18},{18... | collective-permute-start | bytes 196616 | tf_op jit(solution)/shard_map/ppermute | solution.py:23
  86.4 3.0 %collective-permute-start.19 = (f32[16,16]{1,0:T(8,128)S(1)}, f32[16,16]{1,0:T(8,128)S(1)}, u32[]{:S(2)}, u32[]{:S(2)}) collective-permute-start(f32[16,16]{1,0:T(8,128)S(1)} %fusion.246), channel_id=1, source_target_pairs={{0,1},{2,3},{4,5},{6,7},{8,9},{10,11},{12,13},{14,15},{16,17},{18,... | collective-permute-start | bytes 3080 | tf_op jit(solution)/shard_map/ppermute | solution.py:12
  94.1 5.2 %collective-permute-start.21 = (f32[64,256]{1,0:T(8,128)S(1)}, f32[64,256]{1,0:T(8,128)S(1)}, u32[]{:S(2)}, u32[]{:S(2)}) collective-permute-start(f32[64,256]{1,0:T(8,128)S(1)} %select_select_fusion), channel_id=1, source_target_pairs={{0,2},{2,4},{4,6},{6,8},{8,10},{10,12},{12,14},{14,16},{16,18},{18... | collective-permute-start | bytes 196616 | tf_op jit(solution)/shard_map/ppermute | solution.py:23
  101.2 7.1 %collective-permute-start.22 = (f32[64,256]{1,0:T(8,128)S(1)}, f32[64,256]{1,0:T(8,128)S(1)}, u32[]{:S(2)}, u32[]{:S(2)}) collective-permute-start(f32[64,256]{1,0:T(8,128)S(1)} %broadcast_select_fusion.4), channel_id=1, source_target_pairs={{0,4},{2,6},{4,8},{6,10},{8,12},{10,14},{12,16},{14,18},{16,20},{1... | collective-permute-start | bytes 196616 | tf_op jit(solution)/shard_map/ppermute | solution.py:23
  110.3 51.2 %while.11 = (s32[]{:T(128)}, f32[64,256]{1,0:T(8,128)S(1)}, bf16[3,64,64,256]{3,2,1,0:T(8,128)(2,1)}, f32[64,256]{1,0:T(8,128)S(1)}, f32[2,256,16]{1,2,0:T(8,128...) while((s32[]{:T(128)}, f32[64,256]{1,0:T(8,128)S(1)}, ...), condition=%wide.region_9.10_spmd.clone, body=%wide.region_7.9_spmd.clone.sunk | while | flops 109826336 | bytes 4098933 | solution.py:130
  110.3 9.7 %collective-permute-start = (f32[64,256]{1,0:T(8,128)S(1)}, f32[64,256]{1,0:T(8,128)S(1)}, u32[]{:S(2)}, u32[]{:S(2)}) collective-permute-start(f32[64,256]{1,0:T(8,128)S(1)} %get-tuple-element.256), channel_id=1, source_target_pairs={{0,8},{2,10},{4,12},{6,14},{8,16},{10,18},{12,20},{14,22},{16,24},... | collective-permute-start | bytes 196616 | tf_op jit(solution)/shard_map/while/body/eval_jaxpr/ppermute | solution.py:23
  131.0 4.3 %collective-permute-start = (f32[64,256]{1,0:T(8,128)S(1)}, f32[64,256]{1,0:T(8,128)S(1)}, u32[]{:S(2)}, u32[]{:S(2)}) collective-permute-start(f32[64,256]{1,0:T(8,128)S(1)} %get-tuple-element.256), channel_id=1, source_target_pairs={{0,8},{2,10},{4,12},{6,14},{8,16},{10,18},{12,20},{14,22},{16,24},... | collective-permute-start | bytes 196616 | tf_op jit(solution)/shard_map/while/body/eval_jaxpr/ppermute | solution.py:23
  146.2 4.3 %collective-permute-start = (f32[64,256]{1,0:T(8,128)S(1)}, f32[64,256]{1,0:T(8,128)S(1)}, u32[]{:S(2)}, u32[]{:S(2)}) collective-permute-start(f32[64,256]{1,0:T(8,128)S(1)} %get-tuple-element.256), channel_id=1, source_target_pairs={{0,8},{2,10},{4,12},{6,14},{8,16},{10,18},{12,20},{14,22},{16,24},... | collective-permute-start | bytes 196616 | tf_op jit(solution)/shard_map/while/body/eval_jaxpr/ppermute | solution.py:23
  163.2 3.0 %collective-permute-start.23 = (f32[16,16]{1,0:T(8,128)S(1)}, f32[16,16]{1,0:T(8,128)S(1)}, u32[]{:S(2)}, u32[]{:S(2)}) collective-permute-start(f32[16,16]{1,0:T(8,128)S(1)} %fusion.245), channel_id=1, source_target_pairs={{0,1},{2,3},{4,5},{6,7},{8,9},{10,11},{12,13},{14,15},{16,17},{18,... | collective-permute-start | bytes 3080 | tf_op jit(solution)/shard_map/ppermute | solution.py:12
  172.5 3.0 %collective-permute-start.25 = (f32[16,16]{1,0:T(8,128)S(1)}, f32[16,16]{1,0:T(8,128)S(1)}, u32[]{:S(2)}, u32[]{:S(2)}) collective-permute-start(f32[16,16]{1,0:T(8,128)S(1)} %fusion.244), channel_id=1, source_target_pairs={{0,1},{2,3},{4,5},{6,7},{8,9},{10,11},{12,13},{14,15},{16,17},{18,... | collective-permute-start | bytes 3080 | tf_op jit(solution)/shard_map/ppermute | solution.py:12
  181.9 3.2 %collective-permute-start.27 = (f32[16,16]{1,0:T(8,128)S(1)}, f32[16,16]{1,0:T(8,128)S(1)}, u32[]{:S(2)}, u32[]{:S(2)}) collective-permute-start(f32[16,16]{1,0:T(8,128)S(1)} %fusion.243), channel_id=1, source_target_pairs={{0,1},{2,3},{4,5},{6,7},{8,9},{10,11},{12,13},{14,15},{16,17},{18,... | collective-permute-start | bytes 3080 | tf_op jit(solution)/shard_map/ppermute | solution.py:12
  191.3 3.0 %collective-permute-start.29 = (f32[16,16]{1,0:T(8,128)S(1)}, f32[16,16]{1,0:T(8,128)S(1)}, u32[]{:S(2)}, u32[]{:S(2)}) collective-permute-start(f32[16,16]{1,0:T(8,128)S(1)} %fusion.242), channel_id=1, source_target_pairs={{0,1},{2,3},{4,5},{6,7},{8,9},{10,11},{12,13},{14,15},{16,17},{18,... | collective-permute-start | bytes 3080 | tf_op jit(solution)/shard_map/ppermute | solution.py:12
  200.7 3.0 %collective-permute-start.31 = (f32[16,16]{1,0:T(8,128)S(1)}, f32[16,16]{1,0:T(8,128)S(1)}, u32[]{:S(2)}, u32[]{:S(2)}) collective-permute-start(f32[16,16]{1,0:T(8,128)S(1)} %fusion.241), channel_id=1, source_target_pairs={{0,1},{2,3},{4,5},{6,7},{8,9},{10,11},{12,13},{14,15},{16,17},{18,... | collective-permute-start | bytes 3080 | tf_op jit(solution)/shard_map/ppermute | solution.py:12
  210.1 3.0 %collective-permute-start.33 = (f32[16,16]{1,0:T(8,128)S(1)}, f32[16,16]{1,0:T(8,128)S(1)}, u32[]{:S(2)}, u32[]{:S(2)}) collective-permute-start(f32[16,16]{1,0:T(8,128)S(1)} %fusion.240), channel_id=1, source_target_pairs={{0,1},{2,3},{4,5},{6,7},{8,9},{10,11},{12,13},{14,15},{16,17},{18,... | collective-permute-start | bytes 3080 | tf_op jit(solution)/shard_map/ppermute | solution.py:12
  (412 shorter events, 126.6 us)
Async XLA Ops:
  0.9 6.2 %collective-permute-start.3 = (f32[16,16]{1,0:T(8,128)S(1)}, f32[16,16]{1,0:T(8,128)S(1)}, u32[]{:S(2)}, u32[]{:S(2)}) collective-permute-start(f32[16,16]{1,0:T(8,128)S(1)} %fusion.235), channel_id=1, source_target_pairs={{0,1},{2,3},{4,5},{6,7},{8,9},{10,11},{12,13},{14,15},{16,17},{18,... | collective-permute-start | bytes 3080 | tf_op jit(solution)/shard_map/ppermute | solution.py:12
  12.6 4.4 %collective-permute-start.6 = (f32[16,16]{1,0:T(8,128)S(1)}, f32[16,16]{1,0:T(8,128)S(1)}, u32[]{:S(2)}, u32[]{:S(2)}) collective-permute-start(f32[16,16]{1,0:T(8,128)S(1)} %fusion.263), channel_id=1, source_target_pairs={{1,0},{3,2},{5,4},{7,6},{9,8},{11,10},{13,12},{15,14},{17,16},{19,... | collective-permute-start | bytes 3080 | tf_op jit(solution)/shard_map/ppermute | solution.py:15
  13.9 3.8 %collective-permute-start.5 = (f32[16,16]{1,0:T(8,128)S(1)}, f32[16,16]{1,0:T(8,128)S(1)}, u32[]{:S(2)}, u32[]{:S(2)}) collective-permute-start(f32[16,16]{1,0:T(8,128)S(1)} %fusion.251), channel_id=1, source_target_pairs={{0,1},{2,3},{4,5},{6,7},{8,9},{10,11},{12,13},{14,15},{16,17},{18,... | collective-permute-start | bytes 3080 | tf_op jit(solution)/shard_map/ppermute | solution.py:12
  22.0 4.4 %collective-permute-start.8 = (f32[16,16]{1,0:T(8,128)S(1)}, f32[16,16]{1,0:T(8,128)S(1)}, u32[]{:S(2)}, u32[]{:S(2)}) collective-permute-start(f32[16,16]{1,0:T(8,128)S(1)} %fusion.262), channel_id=1, source_target_pairs={{1,0},{3,2},{5,4},{7,6},{9,8},{11,10},{13,12},{15,14},{17,16},{19,... | collective-permute-start | bytes 3080 | tf_op jit(solution)/shard_map/ppermute | solution.py:15
  23.3 3.8 %collective-permute-start.7 = (f32[16,16]{1,0:T(8,128)S(1)}, f32[16,16]{1,0:T(8,128)S(1)}, u32[]{:S(2)}, u32[]{:S(2)}) collective-permute-start(f32[16,16]{1,0:T(8,128)S(1)} %fusion.250), channel_id=1, source_target_pairs={{0,1},{2,3},{4,5},{6,7},{8,9},{10,11},{12,13},{14,15},{16,17},{18,... | collective-permute-start | bytes 3080 | tf_op jit(solution)/shard_map/ppermute | solution.py:12
  31.4 4.4 %collective-permute-start.10 = (f32[16,16]{1,0:T(8,128)S(1)}, f32[16,16]{1,0:T(8,128)S(1)}, u32[]{:S(2)}, u32[]{:S(2)}) collective-permute-start(f32[16,16]{1,0:T(8,128)S(1)} %fusion.261), channel_id=1, source_target_pairs={{1,0},{3,2},{5,4},{7,6},{9,8},{11,10},{13,12},{15,14},{17,16},{19,... | collective-permute-start | bytes 3080 | tf_op jit(solution)/shard_map/ppermute | solution.py:15
  40.3 6.1 %collective-permute-start.11 = (f32[64,256]{1,0:T(8,128)S(1)}, f32[64,256]{1,0:T(8,128)S(1)}, u32[]{:S(2)}, u32[]{:S(2)}) collective-permute-start(f32[64,256]{1,0:T(8,128)S(1)} %fusion.39), channel_id=1, source_target_pairs={{0,2},{2,4},{4,6},{6,8},{8,10},{10,12},{12,14},{14,16},{16,18},{18... | collective-permute-start | bytes 196616 | tf_op jit(solution)/shard_map/ppermute | solution.py:23
  46.5 6.2 %collective-permute-start.12 = (f32[64,256]{1,0:T(8,128)S(1)}, f32[64,256]{1,0:T(8,128)S(1)}, u32[]{:S(2)}, u32[]{:S(2)}) collective-permute-start(f32[64,256]{1,0:T(8,128)S(1)} %get-tuple-element.117), channel_id=1, source_target_pairs={{0,2},{2,4},{4,6},{6,8},{8,10},{10,12},{12,14},{14,16},{16,18},{18... | collective-permute-start | bytes 196616 | tf_op jit(solution)/shard_map/ppermute | solution.py:23
  53.1 4.4 %collective-permute-start.14 = (f32[16,16]{1,0:T(8,128)S(1)}, f32[16,16]{1,0:T(8,128)S(1)}, u32[]{:S(2)}, u32[]{:S(2)}) collective-permute-start(f32[16,16]{1,0:T(8,128)S(1)} %fusion.260), channel_id=1, source_target_pairs={{1,0},{3,2},{5,4},{7,6},{9,8},{11,10},{13,12},{15,14},{17,16},{19,... | collective-permute-start | bytes 3080 | tf_op jit(solution)/shard_map/ppermute | solution.py:15
  62.1 6.2 %collective-permute-start.15 = (f32[64,256]{1,0:T(8,128)S(1)}, f32[64,256]{1,0:T(8,128)S(1)}, u32[]{:S(2)}, u32[]{:S(2)}) collective-permute-start(f32[64,256]{1,0:T(8,128)S(1)} %add_select_fusion.1), channel_id=1, source_target_pairs={{0,2},{2,4},{4,6},{6,8},{8,10},{10,12},{12,14},{14,16},{16,18},{18... | collective-permute-start | bytes 196616 | tf_op jit(solution)/shard_map/ppermute | solution.py:23
  68.7 4.6 %collective-permute-start.17 = (f32[16,16]{1,0:T(8,128)S(1)}, f32[16,16]{1,0:T(8,128)S(1)}, u32[]{:S(2)}, u32[]{:S(2)}) collective-permute-start(f32[16,16]{1,0:T(8,128)S(1)} %fusion.259), channel_id=1, source_target_pairs={{1,0},{3,2},{5,4},{7,6},{9,8},{11,10},{13,12},{15,14},{17,16},{19,... | collective-permute-start | bytes 3080 | tf_op jit(solution)/shard_map/ppermute | solution.py:15
  77.6 7.1 %collective-permute-start.18 = (f32[64,256]{1,0:T(8,128)S(1)}, f32[64,256]{1,0:T(8,128)S(1)}, u32[]{:S(2)}, u32[]{:S(2)}) collective-permute-start(f32[64,256]{1,0:T(8,128)S(1)} %add_select_fusion), channel_id=1, source_target_pairs={{0,2},{2,4},{4,6},{6,8},{8,10},{10,12},{12,14},{14,16},{16,18},{18... | collective-permute-start | bytes 196616 | tf_op jit(solution)/shard_map/ppermute | solution.py:23
  85.1 4.4 %collective-permute-start.20 = (f32[16,16]{1,0:T(8,128)S(1)}, f32[16,16]{1,0:T(8,128)S(1)}, u32[]{:S(2)}, u32[]{:S(2)}) collective-permute-start(f32[16,16]{1,0:T(8,128)S(1)} %fusion.258), channel_id=1, source_target_pairs={{1,0},{3,2},{5,4},{7,6},{9,8},{11,10},{13,12},{15,14},{17,16},{19,... | collective-permute-start | bytes 3080 | tf_op jit(solution)/shard_map/ppermute | solution.py:15
  94.1 7.1 %collective-permute-start.21 = (f32[64,256]{1,0:T(8,128)S(1)}, f32[64,256]{1,0:T(8,128)S(1)}, u32[]{:S(2)}, u32[]{:S(2)}) collective-permute-start(f32[64,256]{1,0:T(8,128)S(1)} %select_select_fusion), channel_id=1, source_target_pairs={{0,2},{2,4},{4,6},{6,8},{8,10},{10,12},{12,14},{14,16},{16,18},{18... | collective-permute-start | bytes 196616 | tf_op jit(solution)/shard_map/ppermute | solution.py:23
  101.2 9.0 %collective-permute-start.22 = (f32[64,256]{1,0:T(8,128)S(1)}, f32[64,256]{1,0:T(8,128)S(1)}, u32[]{:S(2)}, u32[]{:S(2)}) collective-permute-start(f32[64,256]{1,0:T(8,128)S(1)} %broadcast_select_fusion.4), channel_id=1, source_target_pairs={{0,4},{2,6},{4,8},{6,10},{8,12},{10,14},{12,16},{14,18},{16,20},{1... | collective-permute-start | bytes 196616 | tf_op jit(solution)/shard_map/ppermute | solution.py:23
  110.3 11.6 %collective-permute-start = (f32[64,256]{1,0:T(8,128)S(1)}, f32[64,256]{1,0:T(8,128)S(1)}, u32[]{:S(2)}, u32[]{:S(2)}) collective-permute-start(f32[64,256]{1,0:T(8,128)S(1)} %get-tuple-element.256), channel_id=1, source_target_pairs={{0,8},{2,10},{4,12},{6,14},{8,16},{10,18},{12,20},{14,22},{16,24},... | collective-permute-start | bytes 196616 | tf_op jit(solution)/shard_map/while/body/eval_jaxpr/ppermute | solution.py:23
  131.0 6.2 %collective-permute-start = (f32[64,256]{1,0:T(8,128)S(1)}, f32[64,256]{1,0:T(8,128)S(1)}, u32[]{:S(2)}, u32[]{:S(2)}) collective-permute-start(f32[64,256]{1,0:T(8,128)S(1)} %get-tuple-element.256), channel_id=1, source_target_pairs={{0,8},{2,10},{4,12},{6,14},{8,16},{10,18},{12,20},{14,22},{16,24},... | collective-permute-start | bytes 196616 | tf_op jit(solution)/shard_map/while/body/eval_jaxpr/ppermute | solution.py:23
  146.2 6.2 %collective-permute-start = (f32[64,256]{1,0:T(8,128)S(1)}, f32[64,256]{1,0:T(8,128)S(1)}, u32[]{:S(2)}, u32[]{:S(2)}) collective-permute-start(f32[64,256]{1,0:T(8,128)S(1)} %get-tuple-element.256), channel_id=1, source_target_pairs={{0,8},{2,10},{4,12},{6,14},{8,16},{10,18},{12,20},{14,22},{16,24},... | collective-permute-start | bytes 196616 | tf_op jit(solution)/shard_map/while/body/eval_jaxpr/ppermute | solution.py:23
  161.9 4.4 %collective-permute-start.24 = (f32[16,16]{1,0:T(8,128)S(1)}, f32[16,16]{1,0:T(8,128)S(1)}, u32[]{:S(2)}, u32[]{:S(2)}) collective-permute-start(f32[16,16]{1,0:T(8,128)S(1)} %fusion.257), channel_id=1, source_target_pairs={{1,0},{3,2},{5,4},{7,6},{9,8},{11,10},{13,12},{15,14},{17,16},{19,... | collective-permute-start | bytes 3080 | tf_op jit(solution)/shard_map/ppermute | solution.py:15
  171.2 4.4 %collective-permute-start.26 = (f32[16,16]{1,0:T(8,128)S(1)}, f32[16,16]{1,0:T(8,128)S(1)}, u32[]{:S(2)}, u32[]{:S(2)}) collective-permute-start(f32[16,16]{1,0:T(8,128)S(1)} %fusion.256), channel_id=1, source_target_pairs={{1,0},{3,2},{5,4},{7,6},{9,8},{11,10},{13,12},{15,14},{17,16},{19,... | collective-permute-start | bytes 3080 | tf_op jit(solution)/shard_map/ppermute | solution.py:15
  180.6 4.6 %collective-permute-start.28 = (f32[16,16]{1,0:T(8,128)S(1)}, f32[16,16]{1,0:T(8,128)S(1)}, u32[]{:S(2)}, u32[]{:S(2)}) collective-permute-start(f32[16,16]{1,0:T(8,128)S(1)} %fusion.255), channel_id=1, source_target_pairs={{1,0},{3,2},{5,4},{7,6},{9,8},{11,10},{13,12},{15,14},{17,16},{19,... | collective-permute-start | bytes 3080 | tf_op jit(solution)/shard_map/ppermute | solution.py:15
  190.0 4.4 %collective-permute-start.30 = (f32[16,16]{1,0:T(8,128)S(1)}, f32[16,16]{1,0:T(8,128)S(1)}, u32[]{:S(2)}, u32[]{:S(2)}) collective-permute-start(f32[16,16]{1,0:T(8,128)S(1)} %fusion.254), channel_id=1, source_target_pairs={{1,0},{3,2},{5,4},{7,6},{9,8},{11,10},{13,12},{15,14},{17,16},{19,... | collective-permute-start | bytes 3080 | tf_op jit(solution)/shard_map/ppermute | solution.py:15
  199.4 4.4 %collective-permute-start.32 = (f32[16,16]{1,0:T(8,128)S(1)}, f32[16,16]{1,0:T(8,128)S(1)}, u32[]{:S(2)}, u32[]{:S(2)}) collective-permute-start(f32[16,16]{1,0:T(8,128)S(1)} %fusion.253), channel_id=1, source_target_pairs={{1,0},{3,2},{5,4},{7,6},{9,8},{11,10},{13,12},{15,14},{17,16},{19,... | collective-permute-start | bytes 3080 | tf_op jit(solution)/shard_map/ppermute | solution.py:15
  208.8 4.4 %collective-permute-start.34 = (f32[16,16]{1,0:T(8,128)S(1)}, f32[16,16]{1,0:T(8,128)S(1)}, u32[]{:S(2)}, u32[]{:S(2)}) collective-permute-start(f32[16,16]{1,0:T(8,128)S(1)} %fusion.252), channel_id=1, source_target_pairs={{1,0},{3,2},{5,4},{7,6},{9,8},{11,10},{13,12},{15,14},{17,16},{19,... | collective-permute-start | bytes 3080 | tf_op jit(solution)/shard_map/ppermute | solution.py:15
  (22 other events, 162.5 us)
where the time goes:
time: 220 us; the launch traced here: 219 us
  starting transfers between devices  112 us (51%)
  other arithmetic  45.7 us (21%)
  waiting for transfers between devices  29.9 us (14%)
  matrix products  24.5 us (11%)
  local copies, waits for them, and re-layouts  4.1 us (2%)
    ppermute x9, starting transfers between devices, from_behind(): lax.ppermute(value, axis, [(source, source + steps) for source in range(i...  48.6 us
    ppermute x16, starting transfers between devices, extended_2(): lax.ppermute(lax.slice_in_dim(block, block.shape[dim] - width, None, axis...  43 us
    reduce_sum x16, other arithmetic, propagate(): return jnp.sum(inverse * rhs_local[None, :, :], axis=1)  36.8 us
    ppermute x16, starting transfers between devices, extended_2(): lax.ppermute(lax.slice_in_dim(block, 0, width, axis=dim), axis, backward)  20.8 us
    ppermute x9, waiting for transfers between devices, from_behind(): lax.ppermute(value, axis, [(source, source + steps) for source in range(i...  16.1 us
    dot_general x16, matrix products, propagate(): jnp.einsum('fkw,fwe->fke', extended, picker, precision=lax.Precision.HIGH...  14.1 us
    ppermute x16, waiting for transfers between devices, extended_2(): lax.ppermute(lax.slice_in_dim(block, block.shape[dim] - width, None, axis...  8.68 us
    ppermute x16, waiting for transfers between devices, extended_2(): lax.ppermute(lax.slice_in_dim(block, 0, width, axis=dim), axis, backward)  5.17 us
  transfers between devices with their start and end apart: 41, of which 24 were waited for; matrix products, arithmetic and copies ran while one was open for 2% of the time, Pallas kernels for 0%

commit v1 on v0

v1 whole, which is shorter than its diff:
```python
import functools
import jax
import jax.numpy as jnp
from jax import lax
from jax.experimental import pallas as pl
from jax.experimental.pallas import tpu as pltpu
from jax.sharding import PartitionSpec as P

MESH = pl.DeviceIdType.MESH
HI = lax.Precision.HIGHEST


def lane_take(block, index):
    return jnp.take_along_axis(block, index, axis=1, mode="promise_in_bounds")


def kernel(tm_size, space_size, source, initial, mass, inverses, couplings, neighbours, sends,
           out, inv, tables, state, traces, halo, rhs, low, high, slots, picks, where_halo,
           next_source, r_all, w_in, w_out,
           inv_sem, halo_send, halo_recv, slot_send, slot_recv, src_send, src_recv,
           r_send, r_recv, w_send, w_recv):
    f32 = jnp.float32
    d = lax.axis_index("tm")
    k = lax.axis_index("space")
    j = lax.rem(d, 4)
    m = lax.div(d, 4)
    groups = tm_size // 4
    above = lax.rem(k + 1, space_size)
    below = lax.rem(k + space_size - 1, space_size)
    peers = [4 * m + lax.rem(j + step, 4) for step in (1, 2, 3)]

    loads = [pltpu.make_async_copy(inverses.at[l], inv.at[l], inv_sem.at[l]) for l in range(3)]
    loads[0].start()
    loads[1].start()
    loads[2].start()

    barrier = pltpu.get_barrier_semaphore()

    def greet(t, s):
        pl.semaphore_signal(barrier, inc=1, device_id=(t, s), device_id_type=MESH)

    greet(d, above)
    greet(d, below)
    for peer in peers:
        greet(peer, k)

    @pl.when(d > 0)
    def _():
        greet(d - 1, k)

    @pl.when(d < tm_size - 1)
    def _():
        greet(d + 1, k)

    @pl.when(m > 0)
    def _():
        greet(d - 4, k)

    @pl.when(m < groups - 1)
    def _():
        greet(d + 4, k)

    slots[0] = jnp.zeros((8, 128), jnp.int32)
    slots[0, 0:2, 0:16] = sends[...]

    n = lax.broadcasted_iota(jnp.int32, (64, 96), 0)
    col = lax.broadcasted_iota(jnp.int32, (64, 96), 1)
    a, b, c = n & 3, (n >> 2) & 3, n >> 4
    face, point = col >> 4, col & 15
    axis = face >> 1
    fixed = jnp.where(axis == 0, a, jnp.where(axis == 1, b, c))
    place = jnp.where(axis == 0, b + 4 * c, jnp.where(axis == 1, a + 4 * c, a + 4 * b))
    lift = ((fixed == 3 * (face & 1)) & (place == point)).astype(f32)
    spread = (lax.broadcasted_iota(jnp.int32, (16, 96), 0)
              == (lax.broadcasted_iota(jnp.int32, (16, 96), 1) & 15)).astype(f32)
    same = (lax.broadcasted_iota(jnp.int32, (96, 96), 0) >> 4
            == lax.broadcasted_iota(jnp.int32, (96, 96), 1) >> 4)
    for l in range(3):
        wide = jnp.dot(couplings[l], spread, precision=HI, preferred_element_type=f32)
        tables[l] = jnp.dot(lift, jnp.where(same, wide, 0.0), precision=HI,
                            preferred_element_type=f32)

    nb = neighbours[...]
    picks[...] = jnp.where(nb < 256, nb, 512)

    pl.semaphore_wait(
        barrier,
        5 + (d > 0).astype(jnp.int32) + (d < tm_size - 1).astype(jnp.int32)
        + (m > 0).astype(jnp.int32) + (m < groups - 1).astype(jnp.int32))

    lists = [
        pltpu.make_async_remote_copy(slots.at[0], slots.at[1], slot_send.at[0], slot_recv.at[0],
                                     device_id=(d, above), device_id_type=MESH),
        pltpu.make_async_remote_copy(slots.at[0], slots.at[2], slot_send.at[1], slot_recv.at[1],
                                     device_id=(d, below), device_id_type=MESH)]
    for copy in lists:
        copy.start()

    back = jnp.maximum(d - 1, 0)
    forth = jnp.where(d > 0, d - 1, 1)
    ahead = pltpu.make_async_remote_copy(source.at[0], next_source, src_send, src_recv,
                                         device_id=(forth, k), device_id_type=MESH)

    @pl.when(d > 0)
    def _():
        ahead.start()

    @pl.when(d == tm_size - 1)
    def _():
        next_source[...] = jnp.zeros_like(next_source)

    for copy in lists:
        copy.wait()
    for row, (held, line, begin, exists) in enumerate(
            [(1, 1, 256, k > 0), (2, 0, 272, k < space_size - 1)]):
        for tile in (0, 1):
            lanes = pl.ds(128 * tile, 128)
            entry = jnp.broadcast_to(neighbours[row:row + 1, lanes], (8, 128)) - begin
            listed = jnp.broadcast_to(slots[held, line:line + 1, :], (8, 128))
            taken = lane_take(listed, jnp.clip(entry, 0, 15))
            limit = jnp.where(exists, 16, 0)
            valid = (entry >= 0) & (entry < limit)
            where_halo[row, :, lanes] = jnp.where(valid, taken, 512)

    def take_from(block, index_of):
        halves = []
        for tile in (0, 1):
            index = index_of(tile)
            spot = index & 127
            part = index >> 7
            halves.append(jnp.where(part == 0, lane_take(block[:, :128], spot),
                                    jnp.where(part == 1, lane_take(block[:, 128:], spot), 0.0)))
        return jnp.concatenate(halves, axis=1)

    def across(ref, begin, size, stride=None):
        return jnp.concatenate([ref[tile, pl.ds(begin, size, stride), :] for tile in (0, 1)], axis=1)

    def phi(level, slot, value):
        for tile in (0, 1):
            state[tile] = value[:, 128 * tile:128 * tile + 128]
        traces[slot, 0] = across(state, 0, 16, 4)
        traces[slot, 1] = across(state, 3, 16, 4)
        moves = [
            pltpu.make_async_remote_copy(traces.at[slot, 1], halo.at[slot, 0], halo_send.at[slot, 0],
                                         halo_recv.at[slot, 0], device_id=(d, above),
                                         device_id_type=MESH),
            pltpu.make_async_remote_copy(traces.at[slot, 0], halo.at[slot, 1], halo_send.at[slot, 1],
                                         halo_recv.at[slot, 1], device_id=(d, below),
                                         device_id_type=MESH)]
        for move in moves:
            move.start()
        faces = [
            traces[slot, 0], traces[slot, 1],
            jnp.concatenate([value[16 * q:16 * q + 4, :] for q in range(4)], axis=0),
            jnp.concatenate([value[16 * q + 12:16 * q + 16, :] for q in range(4)], axis=0),
            value[0:16, :], value[48:64, :]]
        picked = jnp.concatenate(
            [take_from(faces[f ^ 1], lambda tile, f=f: jnp.broadcast_to(
                picks[f:f + 1, 128 * tile:128 * tile + 128], (16, 128))) for f in range(6)], axis=0)
        coupled = jnp.dot(tables[level], picked, precision=HI, preferred_element_type=f32)
        known = mass[...] * value - coupled
        for tile in (0, 1):
            rhs[tile] = known[:, 128 * tile:128 * tile + 128]

        def early(q, total):
            for step in (1, 2):
                at = 4 * q + step
                total = total + inv[level, at].astype(f32) * across(rhs, at, 1)
            return total

        total = lax.fori_loop(0, 16, early, jnp.zeros((64, 256), f32), unroll=2)
        for move in moves:
            move.wait()
        for row, kept, first in ((0, low, 0), (1, high, 3)):
            got = take_from(halo[slot, row], lambda tile, row=row: jnp.concatenate(
                [where_halo[row, :, 128 * tile:128 * tile + 128]] * 2, axis=0))
            change = jnp.dot(couplings[level, 16 * row:16 * row + 16, :], got, precision=HI,
                             preferred_element_type=f32)
            kept[...] = across(rhs, first, 16, 4) - change

        def late(q, total):
            total = total + inv[level, 4 * q].astype(f32) * low[pl.ds(q, 1), :]
            return total + inv[level, 4 * q + 3].astype(f32) * high[pl.ds(q, 1), :]

        return lax.fori_loop(0, 16, late, total, unroll=2)

    loads[0].wait()
    value = source[1]
    value = phi(0, 0, value) + source[2]
    value = phi(0, 1, value) + source[3]
    value = phi(0, 0, value)

    @pl.when(d < tm_size - 1)
    def _():
        ahead.wait_recv()

    @pl.when(d > 0)
    def _():
        ahead.wait_send()

    r_all[j] = value + next_source[...]
    shares = [pltpu.make_async_remote_copy(r_all.at[j], r_all.at[j], r_send.at[i], r_recv.at[j],
                                           device_id=(peer, k), device_id_type=MESH)
              for i, peer in enumerate(peers)]
    for share in shares:
        share.start()

    def share_arrived(i):
        @pl.when(j != i)
        def _():
            pltpu.make_async_remote_copy(r_all.at[i], r_all.at[i], r_send.at[0], r_recv.at[i],
                                         device_id=(peers[0], k), device_id_type=MESH).wait_recv()

    loads[2].wait()
    first = phi(2, 1, initial[...])
    loads[1].wait()
    share_arrived(0)
    value = phi(1, 0, r_all[0])
    share_arrived(1)
    value = phi(1, 1, value + r_all[1])
    share_arrived(2)
    value = phi(1, 0, value + r_all[2])
    share_arrived(3)
    w_out[...] = value + r_all[3]
    for share in shares:
        share.wait_send()

    onward = pltpu.make_async_remote_copy(w_out, w_in, w_send, w_recv,
                                          device_id=(jnp.where(m < groups - 1, d + 4, d - 4), k),
                                          device_id_type=MESH)

    @pl.when(m == 0)
    def _():
        w_in[...] = initial[...]
        w_out[...] = w_out[...] + first

    @pl.when(m > 0)
    def _():
        onward.wait_recv()

    @pl.when((m > 0) & (m < groups - 1))
    def _():
        w_out[...] = w_out[...] + phi(2, 2, w_in[...])

    @pl.when(m < groups - 1)
    def _():
        onward.start()

    value = w_in[...]
    for i in (1, 2, 3):
        moved = phi(1, i % 2, value) + r_all[i - 1]
        value = jnp.where(j >= i, moved, value)
    out[0] = value
    for i in (1, 2, 3):
        value = phi(0, (i + 1) % 2, value) + source[i]
        out[i] = value

    @pl.when(m < groups - 1)
    def _():
        onward.wait_send()


def local(tm_size, space_size, source, initial, mass, inverses, couplings, neighbours, sends):
    f32 = jnp.float32
    turned = jnp.swapaxes(inverses, 1, 2)
    vmem = pl.BlockSpec(memory_space=pltpu.VMEM)
    dma = pltpu.SemaphoreType.DMA
    return pl.pallas_call(
        functools.partial(kernel, tm_size, space_size),
        out_shape=jax.ShapeDtypeStruct(source.shape, f32),
        in_specs=[vmem, vmem, vmem, pl.BlockSpec(memory_space=pl.ANY), vmem, vmem, vmem],
        out_specs=vmem,
        scratch_shapes=[
            pltpu.VMEM(turned.shape, jnp.bfloat16),
            pltpu.VMEM((3, 64, 96), f32),
            pltpu.VMEM((2, 64, 128), f32),
            pltpu.VMEM((3, 2, 16, 256), f32),
            pltpu.VMEM((3, 2, 16, 256), f32),
            pltpu.VMEM((2, 64, 128), f32),
            pltpu.VMEM((16, 256), f32),
            pltpu.VMEM((16, 256), f32),
            pltpu.VMEM((3, 8, 128), jnp.int32),
            pltpu.VMEM((6, 256), jnp.int32),
            pltpu.VMEM((2, 8, 256), jnp.int32),
            pltpu.VMEM((64, 256), f32),
            pltpu.VMEM((4, 64, 256), f32),
            pltpu.VMEM((64, 256), f32),
            pltpu.VMEM((64, 256), f32),
            dma((3,)), dma((3, 2)), dma((3, 2)), dma((2,)), dma((2,)), dma, dma,
            dma((3,)), dma((4,)), dma, dma,
        ],
        compiler_params=pltpu.CompilerParams(collective_id=0, has_side_effects=True),
        name="cycle",
    )(source, initial, mass, turned, couplings.reshape(3, 96, 16), neighbours, sends)


def solution(mesh):
    placed = (
        P("tm", None, "space"),
        P(None, "space"),
        P(None, "space"),
        P(None, None, None, "space"),
        P(),
        P(None, "space"),
        P(None, "space"),
    )
    return jax.shard_map(
        functools.partial(local, mesh.shape["tm"], mesh.shape["space"]),
        mesh=mesh, in_specs=placed, out_specs=P("tm", None, "space"), check_vma=False)
```

time: 220 us -> 50.9 us (0.23)
  the two profiles are of different devices: /device:TPU:0 before, /device:TPU:31 now
where the time goes in v1:
time: 50.9 us; the launch traced here: 50.7 us
  Pallas kernels  40 us (79%)
  local copies, waits for them, and re-layouts  10.7 us (21%)
    pallas_call x1, Pallas kernels, local(): pl.pallas_call(functools.partial(kernel, tm_size, space_size), out_shape=...  40 us
    unnamed x2, local copies, waits for them, and re-layouts  10.7 us

profile of v1, /device:TPU:31, one launch (start us, length us, event | category | flops | bytes accessed | tf_op | source)
XLA Modules:
  0.0 50.7 jit_solution(14899032414331478735)
XLA Ops:
  0.0 9.0 %copy.10 = bf16[3,64,64,256]{3,1,2,0:T(8,128)(2,1)} copy(bf16[3,64,64,256]{3,2,1,0:T(8,128)(2,1)} %param.10) | data formatting | bytes 12582912 | tf_op args[3]
  9.1 40.0 %cycle.1 = f32[4,64,256]{2,1,0:T(8,128)} custom-call(f32[4,64,256]{2,1,0:T(8,128)} %source.1, f32[64,256]{1,0:T(8,128)} %initial.1, f32[64,256]{1,0:T(8,128)} %mass.1, bf16[3,64,64,256]{3,2,1,0:T(8,128)(2,1)} %bitcast.4, f32[3,96,16]{2,1,0:T(8,128)} %bitcast.5, s32[6,256]{1,0:T(8,128)} %neighbours.1, s32[2,16]{1,0:T(2,128)} %sends.1), custom_call_target="tpu_custom_call" | custom-call | tf_op jit(solution)/shard_map/cycle/pallas_call | solution.py:268
  49.0 1.7 %copy.12 = f32[4,64,256]{2,1,0:T(8,128)} copy(f32[4,64,256]{2,1,0:T(8,128)} %cycle.1) | data formatting | bytes 524288

commit v2 on v1

--- a/solution.py
+++ b/solution.py
@@ -15,7 +15,7 @@
 
 
 def kernel(tm_size, space_size, source, initial, mass, inverses, couplings, neighbours, sends,
-           out, inv, tables, state, traces, halo, rhs, low, high, slots, picks, where_halo,
+           out, packed, stage, inv, tables, state, traces, halo, rhs, low, high, slots, picks, where_halo,
            next_source, r_all, w_in, w_out,
            inv_sem, halo_send, halo_recv, slot_send, slot_recv, src_send, src_recv,
            r_send, r_recv, w_send, w_recv):
@@ -29,7 +29,7 @@
     below = lax.rem(k + space_size - 1, space_size)
     peers = [4 * m + lax.rem(j + step, 4) for step in (1, 2, 3)]
 
-    loads = [pltpu.make_async_copy(inverses.at[l], inv.at[l], inv_sem.at[l]) for l in range(3)]
+    loads = [pltpu.make_async_copy(inverses.at[l], packed.at[l], inv_sem.at[l]) for l in range(3)]
     loads[0].start()
     loads[1].start()
     loads[2].start()
@@ -80,8 +80,27 @@
         tables[l] = jnp.dot(lift, jnp.where(same, wide, 0.0), precision=HI,
                             preferred_element_type=f32)
 
+    def prepare(level, begin, end):
+        def block(part, carry):
+            for i in range(8):
+                whole = packed[level, 8 * part + i].astype(f32)
+                for tile in (0, 1):
+                    stage[tile, 64 * i:64 * i + 64, :] = whole[:, 128 * tile:128 * tile + 128]
+            rows = pl.ds(pl.multiple_of(8 * part, 8), 8)
+            for at in range(64):
+                for tile in (0, 1):
+                    inv[level, at, tile, rows, :] = stage[tile, pl.ds(at, 8, 64), :]
+            return carry
+
+        lax.fori_loop(begin, end, block, 0)
+
     nb = neighbours[...]
     picks[...] = jnp.where(nb < 256, nb, 512)
+
+    loads[0].wait()
+    prepare(0, 0, 8)
+    loads[1].wait()
+    loads[2].wait()
 
     pl.semaphore_wait(
         barrier,
@@ -135,7 +154,7 @@
     def across(ref, begin, size, stride=None):
         return jnp.concatenate([ref[tile, pl.ds(begin, size, stride), :] for tile in (0, 1)], axis=1)
 
-    def phi(level, slot, value):
+    def phi(level, slot, value, meanwhile=None):
         for tile in (0, 1):
             state[tile] = value[:, 128 * tile:128 * tile + 128]
         traces[slot, 0] = across(state, 0, 16, 4)
@@ -165,10 +184,12 @@
         def early(q, total):
             for step in (1, 2):
                 at = 4 * q + step
-                total = total + inv[level, at].astype(f32) * across(rhs, at, 1)
+                total = total + inv[level, at] * rhs[:, pl.ds(at, 1), :]
             return total
 
-        total = lax.fori_loop(0, 16, early, jnp.zeros((64, 256), f32), unroll=2)
+        total = lax.fori_loop(0, 16, early, jnp.zeros((2, 64, 128), f32), unroll=2)
+        if meanwhile is not None:
+            prepare(*meanwhile)
         for move in moves:
             move.wait()
         for row, kept, first in ((0, low, 0), (1, high, 3)):
@@ -176,19 +197,20 @@
                 [where_halo[row, :, 128 * tile:128 * tile + 128]] * 2, axis=0))
             change = jnp.dot(couplings[level, 16 * row:16 * row + 16, :], got, precision=HI,
                              preferred_element_type=f32)
-            kept[...] = across(rhs, first, 16, 4) - change
+            for tile in (0, 1):
+                kept[tile] = rhs[tile, pl.ds(first, 16, 4), :] - change[:, 128 * tile:128 * tile + 128]
 
         def late(q, total):
-            total = total + inv[level, 4 * q].astype(f32) * low[pl.ds(q, 1), :]
-            return total + inv[level, 4 * q + 3].astype(f32) * high[pl.ds(q, 1), :]
-
-        return lax.fori_loop(0, 16, late, total, unroll=2)
-
-    loads[0].wait()
+            total = total + inv[level, 4 * q] * low[:, pl.ds(q, 1), :]
+            return total + inv[level, 4 * q + 3] * high[:, pl.ds(q, 1), :]
+
+        total = lax.fori_loop(0, 16, late, total, unroll=2)
+        return jnp.concatenate([total[0], total[1]], axis=1)
+
     value = source[1]
-    value = phi(0, 0, value) + source[2]
-    value = phi(0, 1, value) + source[3]
-    value = phi(0, 0, value)
+    value = phi(0, 0, value, (1, 0, 3)) + source[2]
+    value = phi(0, 1, value, (1, 3, 6)) + source[3]
+    value = phi(0, 0, value, (1, 6, 8))
 
     @pl.when(d < tm_size - 1)
     def _():
@@ -211,9 +233,8 @@
             pltpu.make_async_remote_copy(r_all.at[i], r_all.at[i], r_send.at[0], r_recv.at[i],
                                          device_id=(peers[0], k), device_id_type=MESH).wait_recv()
 
-    loads[2].wait()
+    prepare(2, 0, 8)
     first = phi(2, 1, initial[...])
-    loads[1].wait()
     share_arrived(0)
     value = phi(1, 0, r_all[0])
     share_arrived(1)
@@ -262,7 +283,6 @@
 
 def local(tm_size, space_size, source, initial, mass, inverses, couplings, neighbours, sends):
     f32 = jnp.float32
-    turned = jnp.swapaxes(inverses, 1, 2)
     vmem = pl.BlockSpec(memory_space=pltpu.VMEM)
     dma = pltpu.SemaphoreType.DMA
     return pl.pallas_call(
@@ -271,14 +291,16 @@
         in_specs=[vmem, vmem, vmem, pl.BlockSpec(memory_space=pl.ANY), vmem, vmem, vmem],
         out_specs=vmem,
         scratch_shapes=[
-            pltpu.VMEM(turned.shape, jnp.bfloat16),
+            pltpu.VMEM(inverses.shape, jnp.bfloat16),
+            pltpu.VMEM((2, 512, 128), f32),
+            pltpu.VMEM((3, 64, 2, 64, 128), f32),
             pltpu.VMEM((3, 64, 96), f32),
             pltpu.VMEM((2, 64, 128), f32),
             pltpu.VMEM((3, 2, 16, 256), f32),
             pltpu.VMEM((3, 2, 16, 256), f32),
             pltpu.VMEM((2, 64, 128), f32),
-            pltpu.VMEM((16, 256), f32),
-            pltpu.VMEM((16, 256), f32),
+            pltpu.VMEM((2, 16, 128), f32),
+            pltpu.VMEM((2, 16, 128), f32),
             pltpu.VMEM((3, 8, 128), jnp.int32),
             pltpu.VMEM((6, 256), jnp.int32),
             pltpu.VMEM((2, 8, 256), jnp.int32),
@@ -291,7 +313,7 @@
         ],
         compiler_params=pltpu.CompilerParams(collective_id=0, has_side_effects=True),
         name="cycle",
-    )(source, initial, mass, turned, couplings.reshape(3, 96, 16), neighbours, sends)
+    )(source, initial, mass, inverses, couplings.reshape(3, 96, 16), neighbours, sends)
 
 
 def solution(mesh):

time: 50.9 us -> 44.3 us (0.87)
  local copies, waits for them, and re-layouts: 10.7 us -> 1.67 us
  Pallas kernels: 40 us -> 42.5 us
    unnamed x2 -> x1, local copies, waits for them, and re-layouts: 10.7 us -> 1.67 us
    pallas_call x1, Pallas kernels: 40 us -> 42.5 us  [local(): pl.pallas_call(functools.partial(kernel, tm_size, space_size), out_shape=...]
where the time goes in v2:
time: 44.3 us; the launch traced here: 44.2 us
  Pallas kernels  42.5 us (96%)
  local copies, waits for them, and re-layouts  1.67 us (4%)
    pallas_call x1, Pallas kernels, local(): pl.pallas_call(functools.partial(kernel, tm_size, space_size), out_shape=...  42.5 us
    unnamed x1, local copies, waits for them, and re-layouts  1.67 us

profile of v2, /device:TPU:31, one launch (start us, length us, event | category | flops | bytes accessed | tf_op | source)
XLA Modules:
  0.0 44.2 jit_solution(11096507167943586417)
XLA Ops:
  0.0 42.5 %cycle.1 = f32[4,64,256]{2,1,0:T(8,128)} custom-call(f32[4,64,256]{2,1,0:T(8,128)} %source.1, f32[64,256]{1,0:T(8,128)} %initial.1, f32[64,256]{1,0:T(8,128)} %mass.1, bf16[3,64,64,256]{3,2,1,0:T(8,128)(2,1)} %inverses.1, f32[3,96,16]{2,1,0:T(8,128)} %bitcast.1, s32[6,256]{1,0:T(8,128)} %neighbours.1, s32[2,16]{1,0:T(2,128)} %sends.1), custom_call_target="tpu_custom_call" | custom-call | tf_op jit(solution)/shard_map/cycle/pallas_call | solution.py:288
  42.5 1.7 %copy.9 = f32[4,64,256]{2,1,0:T(8,128)} copy(f32[4,64,256]{2,1,0:T(8,128)} %cycle.1) | data formatting | bytes 524288

commit v3 on v2

--- a/solution.py
+++ b/solution.py
@@ -15,7 +15,7 @@
 
 
 def kernel(tm_size, space_size, source, initial, mass, inverses, couplings, neighbours, sends,
-           out, packed, stage, inv, tables, state, traces, halo, rhs, low, high, slots, picks, where_halo,
+           out, packed, stage, inv, tables, edges, state, traces, halo, rhs, low, high, slots, picks, where_halo,
            next_source, r_all, w_in, w_out,
            inv_sem, halo_send, halo_recv, slot_send, slot_recv, src_send, src_recv,
            r_send, r_recv, w_send, w_recv):
@@ -75,21 +75,36 @@
               == (lax.broadcasted_iota(jnp.int32, (16, 96), 1) & 15)).astype(f32)
     same = (lax.broadcasted_iota(jnp.int32, (96, 96), 0) >> 4
             == lax.broadcasted_iota(jnp.int32, (96, 96), 1) >> 4)
+    def split(x):
+        top = x.astype(jnp.bfloat16)
+        return top, (x - top.astype(f32)).astype(jnp.bfloat16)
+
+    def stacked(x):
+        top, rest = split(x)
+        return jnp.concatenate([jnp.concatenate([top, top], axis=1),
+                                jnp.concatenate([rest, rest], axis=1)], axis=0)
+
+    def times(table, x):
+        both = jnp.dot(table, jnp.concatenate(split(x), axis=0), preferred_element_type=f32)
+        half = both.shape[0] // 2
+        return both[:half] + both[half:]
+
     for l in range(3):
         wide = jnp.dot(couplings[l], spread, precision=HI, preferred_element_type=f32)
-        tables[l] = jnp.dot(lift, jnp.where(same, wide, 0.0), precision=HI,
-                            preferred_element_type=f32)
+        tables[l] = stacked(jnp.dot(lift, jnp.where(same, wide, 0.0), precision=HI,
+                                    preferred_element_type=f32))
+        edges[l] = stacked(jnp.where(same, wide, 0.0)[:32, :32])
 
     def prepare(level, begin, end):
         def block(part, carry):
             for i in range(8):
                 whole = packed[level, 8 * part + i].astype(f32)
                 for tile in (0, 1):
-                    stage[tile, 64 * i:64 * i + 64, :] = whole[:, 128 * tile:128 * tile + 128]
+                    stage[tile, 72 * i:72 * i + 64, :] = whole[:, 128 * tile:128 * tile + 128]
             rows = pl.ds(pl.multiple_of(8 * part, 8), 8)
             for at in range(64):
                 for tile in (0, 1):
-                    inv[level, at, tile, rows, :] = stage[tile, pl.ds(at, 8, 64), :]
+                    inv[level, at, tile, rows, :] = stage[tile, pl.ds(at, 8, 72), :]
             return carry
 
         lax.fori_loop(begin, end, block, 0)
@@ -176,7 +191,7 @@
         picked = jnp.concatenate(
             [take_from(faces[f ^ 1], lambda tile, f=f: jnp.broadcast_to(
                 picks[f:f + 1, 128 * tile:128 * tile + 128], (16, 128))) for f in range(6)], axis=0)
-        coupled = jnp.dot(tables[level], picked, precision=HI, preferred_element_type=f32)
+        coupled = times(tables[level], picked)
         known = mass[...] * value - coupled
         for tile in (0, 1):
             rhs[tile] = known[:, 128 * tile:128 * tile + 128]
@@ -192,13 +207,15 @@
             prepare(*meanwhile)
         for move in moves:
             move.wait()
+        got = jnp.concatenate(
+            [take_from(halo[slot, row], lambda tile, row=row: jnp.concatenate(
+                [where_halo[row, :, 128 * tile:128 * tile + 128]] * 2, axis=0))
+             for row in (0, 1)], axis=0)
+        change = times(edges[level], got)
         for row, kept, first in ((0, low, 0), (1, high, 3)):
-            got = take_from(halo[slot, row], lambda tile, row=row: jnp.concatenate(
-                [where_halo[row, :, 128 * tile:128 * tile + 128]] * 2, axis=0))
-            change = jnp.dot(couplings[level, 16 * row:16 * row + 16, :], got, precision=HI,
-                             preferred_element_type=f32)
             for tile in (0, 1):
-                kept[tile] = rhs[tile, pl.ds(first, 16, 4), :] - change[:, 128 * tile:128 * tile + 128]
+                kept[tile] = (rhs[tile, pl.ds(first, 16, 4), :]
+                              - change[16 * row:16 * row + 16, 128 * tile:128 * tile + 128])
 
         def late(q, total):
             total = total + inv[level, 4 * q] * low[:, pl.ds(q, 1), :]
@@ -292,9 +309,10 @@
         out_specs=vmem,
         scratch_shapes=[
             pltpu.VMEM(inverses.shape, jnp.bfloat16),
-            pltpu.VMEM((2, 512, 128), f32),
+            pltpu.VMEM((2, 576, 128), f32),
             pltpu.VMEM((3, 64, 2, 64, 128), f32),
-            pltpu.VMEM((3, 64, 96), f32),
+            pltpu.VMEM((3, 128, 192), jnp.bfloat16),
+            pltpu.VMEM((3, 64, 64), jnp.bfloat16),
             pltpu.VMEM((2, 64, 128), f32),
             pltpu.VMEM((3, 2, 16, 256), f32),
             pltpu.VMEM((3, 2, 16, 256), f32),

time: 44.3 us -> 40.4 us (0.912)
  Pallas kernels: 42.5 us -> 38.6 us
    pallas_call x1, Pallas kernels: 42.5 us -> 38.6 us  [local(): pl.pallas_call(functools.partial(kernel, tm_size, space_size), out_shape=...]
where the time goes in v3:
time: 40.4 us; the launch traced here: 40.3 us
  Pallas kernels  38.6 us (96%)
  local copies, waits for them, and re-layouts  1.67 us (4%)
    pallas_call x1, Pallas kernels, local(): pl.pallas_call(functools.partial(kernel, tm_size, space_size), out_shape=...  38.6 us
    unnamed x1, local copies, waits for them, and re-layouts  1.67 us

profile of v3, /device:TPU:31, one launch (start us, length us, event | category | flops | bytes accessed | tf_op | source)
XLA Modules:
  0.0 40.3 jit_solution(4146762231004309985)
XLA Ops:
  0.0 38.6 %cycle.1 = f32[4,64,256]{2,1,0:T(8,128)} custom-call(f32[4,64,256]{2,1,0:T(8,128)} %source.1, f32[64,256]{1,0:T(8,128)} %initial.1, f32[64,256]{1,0:T(8,128)} %mass.1, bf16[3,64,64,256]{3,2,1,0:T(8,128)(2,1)} %inverses.1, f32[3,96,16]{2,1,0:T(8,128)} %bitcast.1, s32[6,256]{1,0:T(8,128)} %neighbours.1, s32[2,16]{1,0:T(2,128)} %sends.1), custom_call_target="tpu_custom_call" | custom-call | tf_op jit(solution)/shard_map/cycle/pallas_call | solution.py:305
  38.6 1.7 %copy.9 = f32[4,64,256]{2,1,0:T(8,128)} copy(f32[4,64,256]{2,1,0:T(8,128)} %cycle.1) | data formatting | bytes 524288

commit v4 on v3

--- a/solution.py
+++ b/solution.py
@@ -16,9 +16,9 @@
 
 def kernel(tm_size, space_size, source, initial, mass, inverses, couplings, neighbours, sends,
            out, packed, stage, inv, tables, edges, state, traces, halo, rhs, low, high, slots, picks, where_halo,
-           next_source, r_all, w_in, w_out,
+           next_source, r_all, w_in, s_all,
            inv_sem, halo_send, halo_recv, slot_send, slot_recv, src_send, src_recv,
-           r_send, r_recv, w_send, w_recv):
+           r_send, r_recv, s_send, s_recv):
     f32 = jnp.float32
     d = lax.axis_index("tm")
     k = lax.axis_index("space")
@@ -52,13 +52,10 @@
     def _():
         greet(d + 1, k)
 
-    @pl.when(m > 0)
-    def _():
-        greet(d - 4, k)
-
-    @pl.when(m < groups - 1)
-    def _():
-        greet(d + 4, k)
+    for t in range(groups):
+        @pl.when(m != t)
+        def _(t=t):
+            greet(4 * t + j, k)
 
     slots[0] = jnp.zeros((8, 128), jnp.int32)
     slots[0, 0:2, 0:16] = sends[...]
@@ -119,8 +116,7 @@
 
     pl.semaphore_wait(
         barrier,
-        5 + (d > 0).astype(jnp.int32) + (d < tm_size - 1).astype(jnp.int32)
-        + (m > 0).astype(jnp.int32) + (m < groups - 1).astype(jnp.int32))
+        4 + groups + (d > 0).astype(jnp.int32) + (d < tm_size - 1).astype(jnp.int32))
 
     lists = [
         pltpu.make_async_remote_copy(slots.at[0], slots.at[1], slot_send.at[0], slot_recv.at[0],
@@ -202,7 +198,7 @@
                 total = total + inv[level, at] * rhs[:, pl.ds(at, 1), :]
             return total
 
-        total = lax.fori_loop(0, 16, early, jnp.zeros((2, 64, 128), f32), unroll=2)
+        total = lax.fori_loop(0, 16, early, jnp.zeros((2, 64, 128), f32), unroll=True)
         if meanwhile is not None:
             prepare(*meanwhile)
         for move in moves:
@@ -221,7 +217,7 @@
             total = total + inv[level, 4 * q] * low[:, pl.ds(q, 1), :]
             return total + inv[level, 4 * q + 3] * high[:, pl.ds(q, 1), :]
 
-        total = lax.fori_loop(0, 16, late, total, unroll=2)
+        total = lax.fori_loop(0, 16, late, total, unroll=True)
         return jnp.concatenate([total[0], total[1]], axis=1)
 
     value = source[1]
@@ -259,30 +255,41 @@
     share_arrived(2)
     value = phi(1, 0, value + r_all[2])
     share_arrived(3)
-    w_out[...] = value + r_all[3]
+    s_all[m] = value + r_all[3] + jnp.where(m == 0, first, 0.0)
+
+    onward = {t: pltpu.make_async_remote_copy(
+        s_all.at[m], s_all.at[m], s_send.at[t], s_recv.at[m],
+        device_id=(jnp.where(m < t, 4 * t + j, lax.rem(d + 4, tm_size)), k), device_id_type=MESH)
+        for t in range(groups - 1, 0, -1)}
+    for t, copy in onward.items():
+        @pl.when(m < t)
+        def _(copy=copy):
+            copy.start()
+
     for share in shares:
         share.wait_send()
 
-    onward = pltpu.make_async_remote_copy(w_out, w_in, w_send, w_recv,
-                                          device_id=(jnp.where(m < groups - 1, d + 4, d - 4), k),
-                                          device_id_type=MESH)
+    def s_arrived(i):
+        pltpu.make_async_remote_copy(s_all.at[i], s_all.at[i], s_send.at[0], s_recv.at[i],
+                                     device_id=(lax.rem(d + 4, tm_size), k),
+                                     device_id_type=MESH).wait_recv()
 
     @pl.when(m == 0)
     def _():
         w_in[...] = initial[...]
-        w_out[...] = w_out[...] + first
 
     @pl.when(m > 0)
     def _():
-        onward.wait_recv()
-
-    @pl.when((m > 0) & (m < groups - 1))
-    def _():
-        w_out[...] = w_out[...] + phi(2, 2, w_in[...])
-
-    @pl.when(m < groups - 1)
-    def _():
-        onward.start()
+        s_arrived(0)
+        w_in[...] = s_all[0]
+
+    def coarse(i, carry):
+        moved = phi(2, 2 + lax.rem(i, 2), w_in[...])
+        s_arrived(i)
+        w_in[...] = moved + s_all[i]
+        return carry
+
+    lax.fori_loop(1, m, coarse, 0)
 
     value = w_in[...]
     for i in (1, 2, 3):
@@ -293,9 +300,10 @@
         value = phi(0, (i + 1) % 2, value) + source[i]
         out[i] = value
 
-    @pl.when(m < groups - 1)
-    def _():
-        onward.wait_send()
+    for t, copy in onward.items():
+        @pl.when(m < t)
+        def _(copy=copy):
+            copy.wait_send()
 
 
 def local(tm_size, space_size, source, initial, mass, inverses, couplings, neighbours, sends):
@@ -314,8 +322,8 @@
             pltpu.VMEM((3, 128, 192), jnp.bfloat16),
             pltpu.VMEM((3, 64, 64), jnp.bfloat16),
             pltpu.VMEM((2, 64, 128), f32),
-            pltpu.VMEM((3, 2, 16, 256), f32),
-            pltpu.VMEM((3, 2, 16, 256), f32),
+            pltpu.VMEM((4, 2, 16, 256), f32),
+            pltpu.VMEM((4, 2, 16, 256), f32),
             pltpu.VMEM((2, 64, 128), f32),
             pltpu.VMEM((2, 16, 128), f32),
             pltpu.VMEM((2, 16, 128), f32),
@@ -325,9 +333,9 @@
             pltpu.VMEM((64, 256), f32),
             pltpu.VMEM((4, 64, 256), f32),
             pltpu.VMEM((64, 256), f32),
-            pltpu.VMEM((64, 256), f32),
-            dma((3,)), dma((3, 2)), dma((3, 2)), dma((2,)), dma((2,)), dma, dma,
-            dma((3,)), dma((4,)), dma, dma,
+            pltpu.VMEM((tm_size // 4, 64, 256), f32),
+            dma((3,)), dma((4, 2)), dma((4, 2)), dma((2,)), dma((2,)), dma, dma,
+            dma((3,)), dma((4,)), dma((tm_size // 4,)), dma((tm_size // 4,)),
         ],
         compiler_params=pltpu.CompilerParams(collective_id=0, has_side_effects=True),
         name="cycle",

time: 40.4 us -> 36.5 us (0.903)
  Pallas kernels: 38.6 us -> 34.6 us
    pallas_call x1, Pallas kernels: 38.6 us -> 34.6 us  [local(): pl.pallas_call(functools.partial(kernel, tm_size, space_size), out_shape=...]
where the time goes in v4:
time: 36.5 us; the launch traced here: 36.3 us
  Pallas kernels  34.6 us (95%)
  local copies, waits for them, and re-layouts  1.67 us (5%)
    pallas_call x1, Pallas kernels, local(): pl.pallas_call(functools.partial(kernel, tm_size, space_size), out_shape=...  34.6 us
    unnamed x1, local copies, waits for them, and re-layouts  1.67 us

profile of v4, /device:TPU:31, one launch (start us, length us, event | category | flops | bytes accessed | tf_op | source)
XLA Modules:
  0.0 36.3 jit_solution(4785603078984618195)
XLA Ops:
  0.0 34.6 %cycle.1 = f32[4,64,256]{2,1,0:T(8,128)} custom-call(f32[4,64,256]{2,1,0:T(8,128)} %source.1, f32[64,256]{1,0:T(8,128)} %initial.1, f32[64,256]{1,0:T(8,128)} %mass.1, bf16[3,64,64,256]{3,2,1,0:T(8,128)(2,1)} %inverses.1, f32[3,96,16]{2,1,0:T(8,128)} %bitcast.1, s32[6,256]{1,0:T(8,128)} %neighbours.1, s32[2,16]{1,0:T(2,128)} %sends.1), custom_call_target="tpu_custom_call" | custom-call | tf_op jit(solution)/shard_map/cycle/pallas_call | solution.py:313
  34.6 1.7 %copy.9 = f32[4,64,256]{2,1,0:T(8,128)} copy(f32[4,64,256]{2,1,0:T(8,128)} %cycle.1) | data formatting | bytes 524288
